TPU v7x, 512 devices: a whole 4x4x16 slice. The times are simulated.
512 devices in a mesh: strip: 128 (over z, x, core), frames: 4 (over y).
Axes of the slice: x: 4, y: 4, z: 16, core: 2. Of those that a mesh axis runs over, the one named last changes fastest.
Arguments:
- frames: float32 [512, 512, 512], P('frames', 'strip'), may hold values from -6 to 6
- kernel: float32 [2, 512, 512], P(None, 'frames', 'strip'), may hold values from -6 to 6
- owner_rank: int32 [4, 128], P('frames'), may hold values from 0 to 127, each once within a row
- block_ids: int32 [512, 16], P('frames'), may hold values from 0 to 63
- block_counts: int32 [512], P('frames'), may hold values from 1 to 16, 4096 in all
Outputs:
- disk_blocks: float32 [128, 64, 4096], P('strip', 'frames')
Inputs may be any that keep to these rules, and one draw needn't show every extreme that they name: `owner_rank`: each row lists every rank of a group once; owner s of a group owns the one frame of rank s. `block_ids`: slots at or beyond a frame's count are unused. `block_counts`: some frame uses all 16 slots.
All inputs are finite; a program needn't handle non-finite values. No bound on the sum of `block_counts` on one device may be relied on, other than what follows from the above.
Results may differ from a plain program's by a relative error of at most 0.0003.
Values sent between devices are 32-bit elements; how exact they have to be, the bound alone decides.
A program may use at most 64 MiB of HBM per device.

v0:
```python
import functools

import jax
import jax.numpy as jnp
import ml_dtypes
import numpy as np
from jax import lax
from jax.experimental import pallas as pl
from jax.experimental.pallas import tpu as pltpu
from jax.sharding import Mesh
from jax.sharding import PartitionSpec as P

DET = 512
HALF = DET // 2
NB = 8
MAXB = 16
Z, X, C, Y = 16, 4, 2, 4
PLANE = X * C
STRIPS = Z * PLANE
STRIP = ("z", "x", "c")
U = 272
AHEAD = 2
F32 = jnp.float32
BF16 = jnp.bfloat16
MESH = pl.DeviceIdType.MESH


def offset_of(k):
    h = Z // 2 - (k + 1) // 2
    return (h * (1 - 2 * (k % 2))) % Z


def halves(table):
    high = table.astype(ml_dtypes.bfloat16)
    low = (table - high.astype(np.float64)).astype(ml_dtypes.bfloat16)
    return high, low


def tables():
    n = np.arange(DET)
    angle = 2.0 * np.pi / DET
    u = np.arange(U)
    used = (u <= HALF).astype(np.float64)[:, None]
    rows = np.concatenate([(-offset_of(k) % Z) * 32 + np.arange(32) for k in range(Z)])
    phase = (u[:, None] * rows[None, :]) % DET * angle
    forward = np.concatenate([np.cos(phase) * used, -np.sin(phase) * used])
    forward = forward.reshape(2 * U, 2, HALF).transpose(1, 0, 2)
    j = np.arange(HALF)
    small = (j[:, None] * j[None, :]) % HALF * (2.0 * angle)
    square = np.concatenate([np.cos(small), np.sin(small)], axis=1)
    turn = np.zeros((8, DET))
    turn[0] = np.concatenate([np.cos(j * angle), np.sin(j * angle)])
    out_rows = np.concatenate([n[0::2], n[1::2]])
    weight = np.where(j == 0, 1.0, 2.0) / (DET * DET)
    back = (out_rows[:, None] * j[None, :]) % DET * angle
    inverse = np.concatenate([np.cos(back) * weight, -np.sin(back) * weight], axis=1)
    jj, cc, xx, zz = np.meshgrid(np.arange(4), np.arange(C), np.arange(X), np.arange(Z), indexing="ij")
    v_in = (4 * (8 * zz + 2 * xx + cc) + jj).reshape(-1)
    v_out = np.concatenate([n[0::2], n[1::2]])
    pick = np.concatenate(
        [(n[None, :] == u[:, None]) * used, (n[None, :] == (-u[:, None]) % DET) * used]
    )
    place = np.concatenate(
        [v_in[:, None] == v_out[None, :], v_in[:, None] == (-v_out[None, :]) % DET]
    )
    wide = np.concatenate([*halves(forward[0]), *halves(forward[1])])
    return (
        wide,
        np.concatenate([*halves(square), *halves(inverse), (0.5 * place).astype(ml_dtypes.bfloat16),
                        pick.astype(ml_dtypes.bfloat16)]),
        turn.astype(np.float32),
    )


def remote(src, dst, send_sem, recv_sem, **where):
    return pltpu.make_async_remote_copy(
        src_ref=src, dst_ref=dst, send_sem=send_sem, recv_sem=recv_sem, device_id=where, device_id_type=MESH
    )


def wait_bytes(view, sem):
    pltpu.make_async_copy(view, view, sem).wait()


def split(value):
    high = value.astype(BF16)
    return high, (value - high.astype(F32)).astype(BF16)


def mul(left, right):
    return jnp.dot(left, right, preferred_element_type=F32)


def body(owner_frame, frames_hbm, kernel_hbm, wide_hbm, square_hbm, turn_hbm, plane,
         frames, staged, mid, rows, kern, wide, square, turn, spec, folded,
         in_sem, tab_sem, send_p, recv_p, send_z, recv_z, send_k, recv_kz, recv_kx, recv_ky, recv_kc):
    z, x, c, y = (lax.axis_index(a) for a in ("z", "x", "c", "y"))
    mine = x * C + c
    load = pltpu.make_async_copy(frames_hbm, frames, in_sem.at[0])
    load.start()
    own_rows = pl.ds(pl.multiple_of(y * 1024 + ((c * X + x) * Z + z) * 8, 8), 8)
    load_kernel = pltpu.make_async_copy(kernel_hbm, kern.at[own_rows], in_sem.at[1])
    load_kernel.start()

    peers = [{"x": (x + p // C) % X, "c": (c + p % C) % C} for p in range(1, PLANE)]
    peers += [{"z": (z + d) % Z} for d in range(1, Z)]
    peers += [{"y": (y + d) % Y} for d in range(1, Y)]
    barrier = pltpu.get_barrier_semaphore()
    for peer in peers:
        pl.semaphore_signal(barrier, inc=1, device_id=peer, device_id_type=MESH)
    pl.semaphore_wait(barrier, len(peers))

    load_kernel.wait()
    for d in range(1, Z):
        remote(kern.at[own_rows], kern.at[own_rows], send_k, recv_kz, z=(z + d) % Z).start()
    load.wait()

    def to_plane(k):
        base = ((z + offset_of(k)) % Z) * PLANE
        for p in range(1, PLANE):
            xx, cc = (x + p // C) % X, (c + p % C) % C
            slot = k * PLANE + p
            staged[slot] = frames[owner_frame[base + xx * C + cc]]
            remote(staged.at[slot], mid.at[k * PLANE + mine], send_p, recv_p.at[k], x=xx, c=cc).start()
        mid[k * PLANE + mine] = frames[owner_frame[base + mine]]

    def from_plane(k):
        wait_bytes(mid.at[pl.ds(k * PLANE, PLANE - 1)], recv_p.at[k])

    def along_z(k):
        piece = pl.ds(k * PLANE, PLANE)
        remote(mid.at[piece], rows.at[piece], send_z, recv_z.at[k // 8], z=(z + offset_of(k)) % Z).start()

    def step(k, carry):
        to_plane(k + AHEAD)
        from_plane(k)
        along_z(k)
        return carry

    for k in range(AHEAD):
        to_plane(k)
    lax.fori_loop(0, 3, step, 0)
    third = pl.ds(pl.multiple_of(y * 1024 + (c * X + x) * 128, 128), 128)
    wait_bytes(kern.at[pl.ds(0, 120)], recv_kz)
    for d in range(1, X):
        remote(kern.at[third], kern.at[third], send_k, recv_kx, x=(x + d) % X).start()
    lax.fori_loop(3, 7, step, 0)
    second = pl.ds(pl.multiple_of(y * 1024 + c * 512, 512), 512)
    wait_bytes(kern.at[pl.ds(0, 384)], recv_kx)
    for d in range(1, Y):
        remote(kern.at[second], kern.at[second], send_k, recv_ky.at[d], y=(y + d) % Y).start()
    remote(kern.at[second], kern.at[second], send_k, recv_kc.at[0], c=1 - c).start()
    lax.fori_loop(7, Z - AHEAD, step, 0)
    from_plane(Z - 2)
    along_z(Z - 2)
    from_plane(Z - 1)
    last = pl.ds((Z - 1) * PLANE, PLANE)
    rows[last] = mid[last]

    loads = [
        pltpu.make_async_copy(wide_hbm, wide, tab_sem.at[0]),
        pltpu.make_async_copy(square_hbm, square, tab_sem.at[1]),
        pltpu.make_async_copy(turn_hbm, turn, tab_sem.at[2]),
    ]
    for table in loads:
        table.start()
    for d in range(1, Y):
        view = kern.at[pl.ds(pl.multiple_of((y + Y - d) % Y * 1024 + c * 512, 512), 512)]
        wait_bytes(view, recv_ky.at[d])
        remote(view, view, send_k, recv_kc.at[d], c=1 - c).start()
    for table in loads:
        table.wait()
    for d in range(Y):
        wait_bytes(kern.at[pl.ds(0, 512)], recv_kc.at[d])

    first = []
    for part in range(2):
        t = jnp.concatenate(
            [
                jnp.concatenate(
                    [kern[pl.ds(yy * 1024 + part * 4 + jj, 128, stride=8), :] for jj in range(4)], axis=0
                )
                for yy in range(Y)
            ],
            axis=1,
        )
        high, low = split(t)
        dims = (((1,), (1,)), ((), ()))
        pick = square[pl.ds(2560, 2 * U), :]
        picked = lax.dot_general(pick, high, dims, preferred_element_type=F32)
        picked = picked + lax.dot_general(pick, low, dims, preferred_element_type=F32)
        first.append(picked)
    for sign in range(2):
        stack = jnp.concatenate([f[sign * U:(sign + 1) * U] for f in first], axis=0)
        high, low = split(stack)
        place = square[pl.ds(1536 + sign * DET, DET), :]
        moved = mul(high, place) + mul(low, place)
        if sign == 0:
            folded[...] = moved
        else:
            folded[pl.ds(0, U), :] += moved[:U]
            folded[pl.ds(U, U), :] -= moved[U:]

    def over_rows(g):
        high, low = split(rows[pl.ds(g * 64, 64)].reshape(HALF, DET))
        w_high = wide[pl.ds(g * 4 * U, 2 * U), :]
        w_low = wide[pl.ds(g * 4 * U + 2 * U, 2 * U), :]
        return mul(w_high, high) + mul(w_high, low) + mul(w_low, high)

    wait_bytes(rows.at[pl.ds(0, 64)], recv_z.at[0])
    spec[...] = over_rows(0)
    wait_bytes(rows.at[pl.ds(0, 56)], recv_z.at[1])
    total = spec[...] + over_rows(1)

    t_high, t_low = square[pl.ds(0, HALF), :], square[pl.ds(HALF, HALF), :]
    tc, ts = turn[0:1, :HALF], turn[0:1, HALF:]

    def square_product(parts):
        high, low = split(jnp.concatenate(parts, axis=0))
        full = mul(high, t_high) + mul(low, t_high) + mul(high, t_low)
        return [(full[i * U:(i + 1) * U, :HALF], full[i * U:(i + 1) * U, HALF:]) for i in range(4)]

    re, im = total[:U], total[U:]
    a_re, a_im = re[:, :HALF] + re[:, HALF:], im[:, :HALF] + im[:, HALF:]
    b_re, b_im = re[:, :HALF] - re[:, HALF:], im[:, :HALF] - im[:, HALF:]
    q = square_product([a_re, a_im, b_re * tc + b_im * ts, b_im * tc - b_re * ts])
    products = []
    for side in range(2):
        f_re = q[2 * side][0] + q[2 * side + 1][1]
        f_im = q[2 * side + 1][0] - q[2 * side][1]
        cols = pl.ds(side * HALF, HALF)
        k_re, k_im = folded[pl.ds(0, U), cols], folded[pl.ds(U, U), cols]
        products += [f_re * k_re - f_im * k_im, f_re * k_im + f_im * k_re]
    q = square_product(products)
    a_re, a_im = q[0][0] - q[1][1], q[1][0] + q[0][1]
    o_re, o_im = q[2][0] - q[3][1], q[3][0] + q[2][1]
    b_re, b_im = o_re * tc - o_im * ts, o_im * tc + o_re * ts
    middle = (a_re[HALF:HALF + 1], b_re[HALF:HALF + 1])
    nyquist = jnp.concatenate([middle[0] + middle[1], middle[0] - middle[1]], axis=1) * (1.0 / (DET * DET))
    a_re, a_im, b_re, b_im = (v[:HALF] for v in (a_re, a_im, b_re, b_im))
    stack = jnp.concatenate(
        [
            jnp.concatenate([a_re + b_re, a_re - b_re], axis=1),
            jnp.concatenate([a_im + b_im, a_im - b_im], axis=1),
        ],
        axis=0,
    )
    high, low = split(stack)
    i_high, i_low = square[pl.ds(512, DET), :], square[pl.ds(1024, DET), :]
    result = mul(i_high, high) + mul(i_high, low) + mul(i_low, high)
    even, odd = result[:HALF] + nyquist, result[HALF:] - nyquist
    for t in range(4):
        plane[t, pl.ds(0, HALF), :] = even[:, t * 128:(t + 1) * 128]
        plane[t, pl.ds(HALF, HALF), :] = odd[:, t * 128:(t + 1) * 128]

    wait_bytes(staged.at[pl.ds(0, 112)], send_p)
    wait_bytes(mid.at[pl.ds(0, 120)], send_z)
    wait_bytes(kern.at[pl.ds(0, 120)], send_k)
    wait_bytes(kern.at[pl.ds(0, 384)], send_k)
    wait_bytes(kern.at[pl.ds(0, 3584)], send_k)


def select(owner_frame, ids, counts, plane, out, slots):
    z, x, c = (lax.axis_index(a) for a in STRIP)
    own = owner_frame[(z * X + x) * C + c]
    count = counts[own]
    left = lax.broadcasted_iota(jnp.int32, (16, 128), 1) < 64
    for m in range(MAXB):
        b = jnp.where(m < count, ids[m, own], 0)
        rb, cb = lax.div(b, NB), lax.rem(b, NB)
        lane_tile, lane_half = lax.div(cb, 2), lax.rem(cb, 2)
        for part in range(2):
            start = pl.multiple_of(lax.rem(rb * 32 + (Z - z) * 16 + part * 16, HALF), 16)
            e = plane[lane_tile, pl.ds(start, 16), :]
            o = plane[lane_tile, pl.ds(start + HALF, 16), :]
            low_pair = jnp.where(left, e, pltpu.roll(o, 64, 1))
            high_pair = jnp.where(left, pltpu.roll(e, 64, 1), o)
            pair = jnp.where(lane_half == 0, low_pair, high_pair)
            slots[pl.ds(m * 32 + part * 16, 16), :] = jnp.where(m < count, pair, 0.0)
    for r in range(32):
        out[:, pl.ds(r * 128, 128)] = slots[pl.ds(r, MAXB, stride=32), :]


def shards(frames, kernel, owner_rank, block_ids, block_counts):
    rank = owner_rank.reshape(-1)
    place = jnp.arange(STRIPS, dtype=jnp.int32)
    owner_frame = jnp.sum(jnp.where(rank[None, :] == place[:, None], place[None, :], 0), axis=1)
    wide, square, turn = tables()
    hbm = pl.BlockSpec(memory_space=pltpu.HBM)
    smem = pl.BlockSpec(memory_space=pltpu.SMEM)
    vmem = pl.BlockSpec(memory_space=pltpu.VMEM)
    dma = pltpu.SemaphoreType.DMA
    strips = (STRIPS, 4, DET)
    def in_hbm(array):
        return pltpu.with_memory_space_constraint(array, pltpu.HBM)

    plane = pl.pallas_call(
        body,
        name="correlate",
        out_shape=pltpu.VMEM((4, DET, 128), F32),
        in_specs=[smem, hbm, hbm, hbm, hbm, hbm],
        out_specs=vmem,
        scratch_shapes=[
            pltpu.VMEM(strips, F32),
            pltpu.VMEM(strips, F32),
            pltpu.VMEM(strips, F32),
            pltpu.VMEM(strips, F32),
            pltpu.VMEM((4096, 128), F32),
            pltpu.VMEM(wide.shape, BF16),
            pltpu.VMEM(square.shape, BF16),
            pltpu.VMEM(turn.shape, F32),
            pltpu.VMEM((2 * U, DET), F32),
            pltpu.VMEM((2 * U, DET), F32),
            dma((2,)), dma((3,)), dma, dma((Z,)), dma, dma((2,)), dma, dma, dma, dma((Y,)), dma((Y,)),
        ],
        compiler_params=pltpu.CompilerParams(
            collective_id=0, has_side_effects=True, vmem_limit_bytes=50 << 20
        ),
    )(
        owner_frame,
        in_hbm(frames),
        in_hbm(kernel.transpose(0, 2, 1).reshape(8, 128)),
        in_hbm(jnp.asarray(wide)),
        in_hbm(jnp.asarray(square)),
        in_hbm(jnp.asarray(turn)),
    )
    result = pl.pallas_call(
        select,
        name="select",
        out_shape=jax.ShapeDtypeStruct((MAXB, 4096), F32),
        in_specs=[smem, smem, smem, vmem],
        out_specs=vmem,
        scratch_shapes=[pltpu.VMEM((MAXB * 32, 128), F32)],
        compiler_params=pltpu.CompilerParams(vmem_limit_bytes=4 << 20),
    )(owner_frame, block_ids.T, block_counts, plane)
    return result[None]


def solution(mesh):
    finer = Mesh(mesh.devices.reshape(Z, X, C, Y), ("z", "x", "c", "y"))
    in_specs = (
        P("y", STRIP, None),
        P(None, "y", STRIP),
        P("y", None),
        P("y", None),
        P("y"),
    )
    return jax.shard_map(
        shards, mesh=finer, in_specs=in_specs, out_specs=P(STRIP, "y", None), check_vma=False
    )
```

profile of v0, /device:TPU:24, one launch (start us, length us, event | category | flops | bytes accessed | tf_op | source)
XLA Modules:
  0.0 75.4 jit_solution(7593260072827321859)
XLA Ops:
  0.0 0.8 %select_reduce_fusion.owner_frame = s32[128]{0:T(128)S(1)} fusion(s32[128]{0:T(128)} %bitcast.8), kind=kLoop, calls=%fused_computation | loop fusion | flops 49024 | bytes 1024 | tf_op jit(solution)/shard_map/reduce_sum | solution.py:287
  0.8 0.0 copy-start
  0.8 0.0 copy-start.1
  0.8 72.8 %correlate.1.plane = f32[4,512,128]{2,1,0:T(8,128)S(1)} custom-call(s32[128]{0:T(128)S(1)} %select_reduce_fusion.owner_frame, f32[128,4,512]{2,1,0:T(4,128)} %frames_hbm.1, f32[8,128]{1,0:T(8,128)} %bitcast.7, bf16[2176,256]{1,0:T(8,128)(2,1)} %constant.8.clone.wide_hbm, bf16[3104,512]{1,0:T(8,128)(2,1)} %constant.9.clone.square_hbm, ...), custom_call_target="tpu_custom_call" | custom-call | tf_op jit(solution)/shard_map/correlate/pallas_call | solution.py:297
  73.6 0.0 copy-done
  73.6 0.0 copy-done.1
  73.6 1.8 %select.1 = f32[16,4096]{1,0:T(8,128)} custom-call(s32[128]{0:T(128)S(1)} %select_reduce_fusion.owner_frame, s32[16,128]{1,0:T(8,128)S(1)} %bitcast.6, s32[128]{0:T(128)S(1)} %copy-done.1, f32[4,512,128]{2,1,0:T(8,128)S(1)} %correlate.1.plane), custom_call_target="tpu_custom_call" | custom-call | tf_op jit(solution)/shard_map/select/pallas_call | solution.py:327
Async XLA Ops:
  0.8 72.9 %copy-start = (s32[128,16]{0,1:T(8,128)S(1)}, s32[128,16]{0,1:T(8,128)}, u32[]{:S(2)}) copy-start(s32[128,16]{0,1:T(8,128)} %param.11) | copy-start | bytes 24580
  0.8 72.9 %copy-start.1 = (s32[128]{0:T(128)S(1)}, s32[128]{0:T(128)}, u32[]{:S(2)}) copy-start(s32[128]{0:T(128)} %counts.1) | copy-start | bytes 1540
where the time goes:
time: 76.1 us; the launch traced here: 75.4 us
  Pallas kernels  74.6 us (98%)
    pallas_call x1, Pallas kernels, shards(): pl.pallas_call(body, name='correlate', out_shape=pltpu.VMEM((4, DET, 128)...  72.8 us
    pallas_call x1, Pallas kernels, shards(): pl.pallas_call(select, name='select', out_shape=jax.ShapeDtypeStruct((MAX...  1.78 us

commit v1 on v0

--- a/solution.py
+++ b/solution.py
@@ -20,6 +20,7 @@
 STRIP = ("z", "x", "c")
 U = 272
 AHEAD = 2
+FAR = 2
 F32 = jnp.float32
 BF16 = jnp.bfloat16
 MESH = pl.DeviceIdType.MESH
@@ -47,7 +48,7 @@
     forward = forward.reshape(2 * U, 2, HALF).transpose(1, 0, 2)
     j = np.arange(HALF)
     small = (j[:, None] * j[None, :]) % HALF * (2.0 * angle)
-    square = np.concatenate([np.cos(small), np.sin(small)], axis=1)
+    square = np.block([[np.cos(small), -np.sin(small)], [np.sin(small), np.cos(small)]])
     turn = np.zeros((8, DET))
     turn[0] = np.concatenate([np.cos(j * angle), np.sin(j * angle)])
     out_rows = np.concatenate([n[0::2], n[1::2]])
@@ -92,8 +93,8 @@
 
 
 def body(owner_frame, frames_hbm, kernel_hbm, wide_hbm, square_hbm, turn_hbm, plane,
-         frames, staged, mid, rows, kern, wide, square, turn, spec, folded,
-         in_sem, tab_sem, send_p, recv_p, send_z, recv_z, send_k, recv_kz, recv_kx, recv_ky, recv_kc):
+         frames, staged, mid, far, rows, kern, wide, square, turn, spec, folded,
+         in_sem, tab_sem, send_p, recv_p, send_z, recv_z, recv_far, recv_out, send_k, recv_kz, recv_kx, recv_ky, recv_kc):
     z, x, c, y = (lax.axis_index(a) for a in ("z", "x", "c", "y"))
     mine = x * C + c
     load = pltpu.make_async_copy(frames_hbm, frames, in_sem.at[0])
@@ -102,8 +103,8 @@
     load_kernel = pltpu.make_async_copy(kernel_hbm, kern.at[own_rows], in_sem.at[1])
     load_kernel.start()
 
-    peers = [{"x": (x + p // C) % X, "c": (c + p % C) % C} for p in range(1, PLANE)]
-    peers += [{"z": (z + d) % Z} for d in range(1, Z)]
+    peers = [{"z": (z + offset_of(k)) % Z} for k in range(Z - 1)]
+    peers += [{"x": (x + p // C) % X, "c": (c + p % C) % C} for p in range(1, PLANE)]
     peers += [{"y": (y + d) % Y} for d in range(1, Y)]
     barrier = pltpu.get_barrier_semaphore()
     for peer in peers:
@@ -114,6 +115,12 @@
     for d in range(1, Z):
         remote(kern.at[own_rows], kern.at[own_rows], send_k, recv_kz, z=(z + d) % Z).start()
     load.wait()
+
+    def far_first(k):
+        there = (z + offset_of(k)) % Z
+        for p in range(PLANE):
+            staged[k * PLANE + p] = frames[owner_frame[there * PLANE + p]]
+        remote(staged.at[pl.ds(k * PLANE, PLANE)], far.at[k], send_z, recv_far.at[k], z=there).start()
 
     def to_plane(k):
         base = ((z + offset_of(k)) % Z) * PLANE
@@ -137,20 +144,22 @@
         along_z(k)
         return carry
 
-    for k in range(AHEAD):
+    for k in range(FAR):
+        far_first(k)
+    for k in range(FAR, FAR + AHEAD):
         to_plane(k)
-    lax.fori_loop(0, 3, step, 0)
+    lax.fori_loop(FAR, 5, step, 0)
     third = pl.ds(pl.multiple_of(y * 1024 + (c * X + x) * 128, 128), 128)
     wait_bytes(kern.at[pl.ds(0, 120)], recv_kz)
     for d in range(1, X):
         remote(kern.at[third], kern.at[third], send_k, recv_kx, x=(x + d) % X).start()
-    lax.fori_loop(3, 7, step, 0)
+    lax.fori_loop(5, 8, step, 0)
     second = pl.ds(pl.multiple_of(y * 1024 + c * 512, 512), 512)
     wait_bytes(kern.at[pl.ds(0, 384)], recv_kx)
     for d in range(1, Y):
         remote(kern.at[second], kern.at[second], send_k, recv_ky.at[d], y=(y + d) % Y).start()
     remote(kern.at[second], kern.at[second], send_k, recv_kc.at[0], c=1 - c).start()
-    lax.fori_loop(7, Z - AHEAD, step, 0)
+    lax.fori_loop(8, Z - AHEAD, step, 0)
     from_plane(Z - 2)
     along_z(Z - 2)
     from_plane(Z - 1)
@@ -168,6 +177,12 @@
         view = kern.at[pl.ds(pl.multiple_of((y + Y - d) % Y * 1024 + c * 512, 512), 512)]
         wait_bytes(view, recv_ky.at[d])
         remote(view, view, send_k, recv_kc.at[d], c=1 - c).start()
+    for k in range(FAR):
+        wait_bytes(far.at[k], recv_far.at[k])
+        for p in range(1, PLANE):
+            xx, cc = (x + p // C) % X, (c + p % C) % C
+            remote(far.at[k, xx * C + cc], rows.at[k * PLANE + mine], send_p, recv_out, x=xx, c=cc).start()
+        rows[k * PLANE + mine] = far[k, mine]
     for table in loads:
         table.wait()
     for d in range(Y):
@@ -186,14 +201,14 @@
         )
         high, low = split(t)
         dims = (((1,), (1,)), ((), ()))
-        pick = square[pl.ds(2560, 2 * U), :]
+        pick = square[pl.ds(3072, 2 * U), :]
         picked = lax.dot_general(pick, high, dims, preferred_element_type=F32)
         picked = picked + lax.dot_general(pick, low, dims, preferred_element_type=F32)
         first.append(picked)
     for sign in range(2):
         stack = jnp.concatenate([f[sign * U:(sign + 1) * U] for f in first], axis=0)
         high, low = split(stack)
-        place = square[pl.ds(1536 + sign * DET, DET), :]
+        place = square[pl.ds(2048 + sign * DET, DET), :]
         moved = mul(high, place) + mul(low, place)
         if sign == 0:
             folded[...] = moved
@@ -207,33 +222,30 @@
         w_low = wide[pl.ds(g * 4 * U + 2 * U, 2 * U), :]
         return mul(w_high, high) + mul(w_high, low) + mul(w_low, high)
 
-    wait_bytes(rows.at[pl.ds(0, 64)], recv_z.at[0])
+    wait_bytes(rows.at[pl.ds(0, FAR * (PLANE - 1))], recv_out)
+    wait_bytes(rows.at[pl.ds(0, 64 - FAR * PLANE)], recv_z.at[0])
     spec[...] = over_rows(0)
     wait_bytes(rows.at[pl.ds(0, 56)], recv_z.at[1])
     total = spec[...] + over_rows(1)
 
-    t_high, t_low = square[pl.ds(0, HALF), :], square[pl.ds(HALF, HALF), :]
+    t_high, t_low = square[pl.ds(0, DET), :], square[pl.ds(DET, DET), :]
     tc, ts = turn[0:1, :HALF], turn[0:1, HALF:]
 
-    def square_product(parts):
-        high, low = split(jnp.concatenate(parts, axis=0))
+    def two(first, second):
+        high, low = split(jnp.concatenate([jnp.concatenate(first, axis=1), jnp.concatenate(second, axis=1)], axis=0))
         full = mul(high, t_high) + mul(low, t_high) + mul(high, t_low)
-        return [(full[i * U:(i + 1) * U, :HALF], full[i * U:(i + 1) * U, HALF:]) for i in range(4)]
+        return full[:U, :HALF], full[:U, HALF:], full[U:, :HALF], full[U:, HALF:]
 
     re, im = total[:U], total[U:]
     a_re, a_im = re[:, :HALF] + re[:, HALF:], im[:, :HALF] + im[:, HALF:]
     b_re, b_im = re[:, :HALF] - re[:, HALF:], im[:, :HALF] - im[:, HALF:]
-    q = square_product([a_re, a_im, b_re * tc + b_im * ts, b_im * tc - b_re * ts])
-    products = []
-    for side in range(2):
-        f_re = q[2 * side][0] + q[2 * side + 1][1]
-        f_im = q[2 * side + 1][0] - q[2 * side][1]
-        cols = pl.ds(side * HALF, HALF)
-        k_re, k_im = folded[pl.ds(0, U), cols], folded[pl.ds(U, U), cols]
-        products += [f_re * k_re - f_im * k_im, f_re * k_im + f_im * k_re]
-    q = square_product(products)
-    a_re, a_im = q[0][0] - q[1][1], q[1][0] + q[0][1]
-    o_re, o_im = q[2][0] - q[3][1], q[3][0] + q[2][1]
+    a_re, a_im, o_re, o_im = two([a_re, a_im], [b_re * tc + b_im * ts, b_im * tc - b_re * ts])
+    k_re, k_im = folded[pl.ds(0, U), pl.ds(0, HALF)], folded[pl.ds(U, U), pl.ds(0, HALF)]
+    l_re, l_im = folded[pl.ds(0, U), pl.ds(HALF, HALF)], folded[pl.ds(U, U), pl.ds(HALF, HALF)]
+    a_im, a_re, o_im, o_re = two(
+        [a_re * k_im + a_im * k_re, a_re * k_re - a_im * k_im],
+        [o_re * l_im + o_im * l_re, o_re * l_re - o_im * l_im],
+    )
     b_re, b_im = o_re * tc - o_im * ts, o_im * tc + o_re * ts
     middle = (a_re[HALF:HALF + 1], b_re[HALF:HALF + 1])
     nyquist = jnp.concatenate([middle[0] + middle[1], middle[0] - middle[1]], axis=1) * (1.0 / (DET * DET))
@@ -246,7 +258,7 @@
         axis=0,
     )
     high, low = split(stack)
-    i_high, i_low = square[pl.ds(512, DET), :], square[pl.ds(1024, DET), :]
+    i_high, i_low = square[pl.ds(1024, DET), :], square[pl.ds(1536, DET), :]
     result = mul(i_high, high) + mul(i_high, low) + mul(i_low, high)
     even, odd = result[:HALF] + nyquist, result[HALF:] - nyquist
     for t in range(4):
@@ -304,6 +316,7 @@
             pltpu.VMEM(strips, F32),
             pltpu.VMEM(strips, F32),
             pltpu.VMEM(strips, F32),
+            pltpu.VMEM((FAR, PLANE, 4, DET), F32),
             pltpu.VMEM(strips, F32),
             pltpu.VMEM((4096, 128), F32),
             pltpu.VMEM(wide.shape, BF16),
@@ -311,7 +324,7 @@
             pltpu.VMEM(turn.shape, F32),
             pltpu.VMEM((2 * U, DET), F32),
             pltpu.VMEM((2 * U, DET), F32),
-            dma((2,)), dma((3,)), dma, dma((Z,)), dma, dma((2,)), dma, dma, dma, dma((Y,)), dma((Y,)),
+            dma((2,)), dma((3,)), dma, dma((Z,)), dma, dma((2,)), dma((FAR,)), dma, dma, dma, dma, dma((Y,)), dma((Y,)),
         ],
         compiler_params=pltpu.CompilerParams(
             collective_id=0, has_side_effects=True, vmem_limit_bytes=50 << 20

time: 76.1 us -> 71.5 us (0.940)
  Pallas kernels: 74.6 us -> 69.9 us
    pallas_call x1, Pallas kernels: 72.8 us -> 68.2 us  [shards(): pl.pallas_call(body, name='correlate', out_shape=pltpu.VMEM((4, DET, 128)...]
where the time goes in v1:
time: 71.5 us; the launch traced here: 70.8 us
  Pallas kernels  69.9 us (98%)
  other arithmetic  0.78 us (1%)
    pallas_call x1, Pallas kernels, shards(): pl.pallas_call(body, name='correlate', out_shape=pltpu.VMEM((4, DET, 128)...  68.2 us
    pallas_call x1, Pallas kernels, shards(): pl.pallas_call(select, name='select', out_shape=jax.ShapeDtypeStruct((MAX...  1.78 us

profile of v1, /device:TPU:24, one launch (start us, length us, event | category | flops | bytes accessed | tf_op | source)
XLA Modules:
  0.0 70.8 jit_solution(3293882049392843802)
XLA Ops:
  0.0 0.0 copy-start.1
  0.0 0.0 copy-start
  0.0 0.8 %select_reduce_fusion.owner_frame = s32[128]{0:T(128)S(1)} fusion(s32[128]{0:T(128)} %bitcast.8), kind=kLoop, calls=%fused_computation | loop fusion | flops 49024 | bytes 1024 | tf_op jit(solution)/shard_map/reduce_sum | solution.py:299
  0.8 68.2 %correlate.1.plane = f32[4,512,128]{2,1,0:T(8,128)S(1)} custom-call(s32[128]{0:T(128)S(1)} %select_reduce_fusion.owner_frame, f32[128,4,512]{2,1,0:T(4,128)} %frames_hbm.1, f32[8,128]{1,0:T(8,128)} %bitcast.7, bf16[2176,256]{1,0:T(8,128)(2,1)} %constant.8.clone.wide_hbm, bf16[3616,512]{1,0:T(8,128)(2,1)} %constant.9.clone.square_hbm, ...), custom_call_target="tpu_custom_call" | custom-call | tf_op jit(solution)/shard_map/correlate/pallas_call | solution.py:309
  69.0 0.0 copy-done.1
  69.0 0.0 copy-done
  69.0 1.8 %select.1 = f32[16,4096]{1,0:T(8,128)} custom-call(s32[128]{0:T(128)S(1)} %select_reduce_fusion.owner_frame, s32[16,128]{1,0:T(8,128)S(1)} %bitcast.6, s32[128]{0:T(128)S(1)} %copy-done.1, f32[4,512,128]{2,1,0:T(8,128)S(1)} %correlate.1.plane), custom_call_target="tpu_custom_call" | custom-call | tf_op jit(solution)/shard_map/select/pallas_call | solution.py:340
Async XLA Ops:
  0.0 69.0 %copy-start.1 = (s32[128]{0:T(128)S(1)}, s32[128]{0:T(128)}, u32[]{:S(2)}) copy-start(s32[128]{0:T(128)} %counts.1) | copy-start | bytes 1540
  0.0 69.0 %copy-start = (s32[128,16]{0,1:T(8,128)S(1)}, s32[128,16]{0,1:T(8,128)}, u32[]{:S(2)}) copy-start(s32[128,16]{0,1:T(8,128)} %param.11) | copy-start | bytes 24580

commit v2 on v1

--- a/solution.py
+++ b/solution.py
@@ -19,16 +19,11 @@
 STRIPS = Z * PLANE
 STRIP = ("z", "x", "c")
 U = 272
-AHEAD = 2
-FAR = 2
+AHEAD = 9
+FAR = (8, 9, 7, 10)
 F32 = jnp.float32
 BF16 = jnp.bfloat16
 MESH = pl.DeviceIdType.MESH
-
-
-def offset_of(k):
-    h = Z // 2 - (k + 1) // 2
-    return (h * (1 - 2 * (k % 2))) % Z
 
 
 def halves(table):
@@ -42,8 +37,7 @@
     angle = 2.0 * np.pi / DET
     u = np.arange(U)
     used = (u <= HALF).astype(np.float64)[:, None]
-    rows = np.concatenate([(-offset_of(k) % Z) * 32 + np.arange(32) for k in range(Z)])
-    phase = (u[:, None] * rows[None, :]) % DET * angle
+    phase = (u[:, None] * n[None, :]) % DET * angle
     forward = np.concatenate([np.cos(phase) * used, -np.sin(phase) * used])
     forward = forward.reshape(2 * U, 2, HALF).transpose(1, 0, 2)
     j = np.arange(HALF)
@@ -97,15 +91,19 @@
          in_sem, tab_sem, send_p, recv_p, send_z, recv_z, recv_far, recv_out, send_k, recv_kz, recv_kx, recv_ky, recv_kc):
     z, x, c, y = (lax.axis_index(a) for a in ("z", "x", "c", "y"))
     mine = x * C + c
+    z_at = [z] + [lax.rem(z + d, Z) for d in range(1, Z)]
+    y_at = [y] + [lax.rem(y + d, Y) for d in range(1, Y)]
+    x_at = [x] + [lax.rem(x + d, X) for d in range(1, X)]
+    plane_at = [(x_at[p // C], (c, 1 - c)[p % C]) for p in range(PLANE)]
     load = pltpu.make_async_copy(frames_hbm, frames, in_sem.at[0])
     load.start()
     own_rows = pl.ds(pl.multiple_of(y * 1024 + ((c * X + x) * Z + z) * 8, 8), 8)
     load_kernel = pltpu.make_async_copy(kernel_hbm, kern.at[own_rows], in_sem.at[1])
     load_kernel.start()
 
-    peers = [{"z": (z + offset_of(k)) % Z} for k in range(Z - 1)]
-    peers += [{"x": (x + p // C) % X, "c": (c + p % C) % C} for p in range(1, PLANE)]
-    peers += [{"y": (y + d) % Y} for d in range(1, Y)]
+    peers = [{"z": z_at[d]} for d in range(1, Z)]
+    peers += [{"x": xx, "c": cc} for xx, cc in plane_at[1:]]
+    peers += [{"y": y_at[d]} for d in range(1, Y)]
     barrier = pltpu.get_barrier_semaphore()
     for peer in peers:
         pl.semaphore_signal(barrier, inc=1, device_id=peer, device_id_type=MESH)
@@ -113,58 +111,79 @@
 
     load_kernel.wait()
     for d in range(1, Z):
-        remote(kern.at[own_rows], kern.at[own_rows], send_k, recv_kz, z=(z + d) % Z).start()
+        remote(kern.at[own_rows], kern.at[own_rows], send_k, recv_kz, z=z_at[d]).start()
     load.wait()
 
     def far_first(k):
-        there = (z + offset_of(k)) % Z
+        there = z_at[FAR[k]]
         for p in range(PLANE):
-            staged[k * PLANE + p] = frames[owner_frame[there * PLANE + p]]
-        remote(staged.at[pl.ds(k * PLANE, PLANE)], far.at[k], send_z, recv_far.at[k], z=there).start()
+            staged[there * PLANE + p] = frames[owner_frame[there * PLANE + p]]
+        remote(staged.at[pl.ds(there * PLANE, PLANE)], far.at[k], send_z, recv_far.at[k], z=there).start()
+
+    def is_near(t):
+        away = (t - z + Z) % Z
+        near = away != FAR[0]
+        for d in FAR[1:]:
+            near = jnp.logical_and(near, away != d)
+        return near
+
+    def target_of(k):
+        i = k % 8
+        return (z + Z + (i + 1) // 2 * (1 - 2 * (i % 2))) % (Z // 2) + Z // 2 * (k // (Z // 2))
 
     def to_plane(k):
-        base = ((z + offset_of(k)) % Z) * PLANE
-        for p in range(1, PLANE):
-            xx, cc = (x + p // C) % X, (c + p % C) % C
-            slot = k * PLANE + p
-            staged[slot] = frames[owner_frame[base + xx * C + cc]]
-            remote(staged.at[slot], mid.at[k * PLANE + mine], send_p, recv_p.at[k], x=xx, c=cc).start()
-        mid[k * PLANE + mine] = frames[owner_frame[base + mine]]
-
-    def from_plane(k):
-        wait_bytes(mid.at[pl.ds(k * PLANE, PLANE - 1)], recv_p.at[k])
-
-    def along_z(k):
-        piece = pl.ds(k * PLANE, PLANE)
-        remote(mid.at[piece], rows.at[piece], send_z, recv_z.at[k // 8], z=(z + offset_of(k)) % Z).start()
-
-    def step(k, carry):
-        to_plane(k + AHEAD)
-        from_plane(k)
-        along_z(k)
+        t = target_of(k)
+
+        @pl.when(is_near(t))
+        def _():
+            for p in range(1, PLANE):
+                xx, cc = plane_at[p]
+                slot = t * PLANE + xx * C + cc
+                staged[slot] = frames[owner_frame[slot]]
+                remote(staged.at[slot], mid.at[t * PLANE + mine], send_p, recv_p.at[t], x=xx, c=cc).start()
+            mid[t * PLANE + mine] = frames[owner_frame[t * PLANE + mine]]
+
+    def onward(k):
+        t = target_of(k)
+
+        @pl.when(is_near(t))
+        def _():
+            piece = pl.ds(t * PLANE, PLANE)
+            wait_bytes(mid.at[pl.ds(t * PLANE, PLANE - 1)], recv_p.at[t])
+            slot = (z - t + Z) % Z
+
+            @pl.when(t != z)
+            def _():
+                target = rows.at[pl.ds(slot * PLANE, PLANE)]
+                remote(mid.at[piece], target, send_z, recv_z.at[slot // 8], z=t).start()
+
+            @pl.when(t == z)
+            def _():
+                rows[pl.ds(0, PLANE)] = mid[piece]
+
+    def step(t, carry):
+        to_plane(t + AHEAD)
+        onward(t)
         return carry
 
-    for k in range(FAR):
+    for k in range(len(FAR)):
         far_first(k)
-    for k in range(FAR, FAR + AHEAD):
-        to_plane(k)
-    lax.fori_loop(FAR, 5, step, 0)
+    for t in range(AHEAD):
+        to_plane(t)
+    lax.fori_loop(0, 2, step, 0)
     third = pl.ds(pl.multiple_of(y * 1024 + (c * X + x) * 128, 128), 128)
     wait_bytes(kern.at[pl.ds(0, 120)], recv_kz)
     for d in range(1, X):
-        remote(kern.at[third], kern.at[third], send_k, recv_kx, x=(x + d) % X).start()
-    lax.fori_loop(5, 8, step, 0)
+        remote(kern.at[third], kern.at[third], send_k, recv_kx, x=x_at[d]).start()
+    lax.fori_loop(2, 4, step, 0)
     second = pl.ds(pl.multiple_of(y * 1024 + c * 512, 512), 512)
     wait_bytes(kern.at[pl.ds(0, 384)], recv_kx)
     for d in range(1, Y):
-        remote(kern.at[second], kern.at[second], send_k, recv_ky.at[d], y=(y + d) % Y).start()
+        remote(kern.at[second], kern.at[second], send_k, recv_ky.at[d], y=y_at[d]).start()
     remote(kern.at[second], kern.at[second], send_k, recv_kc.at[0], c=1 - c).start()
-    lax.fori_loop(8, Z - AHEAD, step, 0)
-    from_plane(Z - 2)
-    along_z(Z - 2)
-    from_plane(Z - 1)
-    last = pl.ds((Z - 1) * PLANE, PLANE)
-    rows[last] = mid[last]
+    lax.fori_loop(4, Z - AHEAD, step, 0)
+    for t in range(Z - AHEAD, Z):
+        onward(t)
 
     loads = [
         pltpu.make_async_copy(wide_hbm, wide, tab_sem.at[0]),
@@ -174,15 +193,16 @@
     for table in loads:
         table.start()
     for d in range(1, Y):
-        view = kern.at[pl.ds(pl.multiple_of((y + Y - d) % Y * 1024 + c * 512, 512), 512)]
+        view = kern.at[pl.ds(pl.multiple_of(y_at[Y - d] * 1024 + c * 512, 512), 512)]
         wait_bytes(view, recv_ky.at[d])
         remote(view, view, send_k, recv_kc.at[d], c=1 - c).start()
-    for k in range(FAR):
+    for k in range(len(FAR)):
+        slot = (Z - FAR[k]) * PLANE + mine
         wait_bytes(far.at[k], recv_far.at[k])
         for p in range(1, PLANE):
-            xx, cc = (x + p // C) % X, (c + p % C) % C
-            remote(far.at[k, xx * C + cc], rows.at[k * PLANE + mine], send_p, recv_out, x=xx, c=cc).start()
-        rows[k * PLANE + mine] = far[k, mine]
+            xx, cc = plane_at[p]
+            remote(far.at[k, xx * C + cc], rows.at[slot], send_p, recv_out, x=xx, c=cc).start()
+        rows[slot] = far[k, mine]
     for table in loads:
         table.wait()
     for d in range(Y):
@@ -222,10 +242,10 @@
         w_low = wide[pl.ds(g * 4 * U + 2 * U, 2 * U), :]
         return mul(w_high, high) + mul(w_high, low) + mul(w_low, high)
 
-    wait_bytes(rows.at[pl.ds(0, FAR * (PLANE - 1))], recv_out)
-    wait_bytes(rows.at[pl.ds(0, 64 - FAR * PLANE)], recv_z.at[0])
+    wait_bytes(rows.at[pl.ds(0, len(FAR) * (PLANE - 1))], recv_out)
+    wait_bytes(rows.at[pl.ds(0, 40)], recv_z.at[0])
     spec[...] = over_rows(0)
-    wait_bytes(rows.at[pl.ds(0, 56)], recv_z.at[1])
+    wait_bytes(rows.at[pl.ds(0, 48)], recv_z.at[1])
     total = spec[...] + over_rows(1)
 
     t_high, t_low = square[pl.ds(0, DET), :], square[pl.ds(DET, DET), :]
@@ -316,7 +336,7 @@
             pltpu.VMEM(strips, F32),
             pltpu.VMEM(strips, F32),
             pltpu.VMEM(strips, F32),
-            pltpu.VMEM((FAR, PLANE, 4, DET), F32),
+            pltpu.VMEM((len(FAR), PLANE, 4, DET), F32),
             pltpu.VMEM(strips, F32),
             pltpu.VMEM((4096, 128), F32),
             pltpu.VMEM(wide.shape, BF16),
@@ -324,7 +344,7 @@
             pltpu.VMEM(turn.shape, F32),
             pltpu.VMEM((2 * U, DET), F32),
             pltpu.VMEM((2 * U, DET), F32),
-            dma((2,)), dma((3,)), dma, dma((Z,)), dma, dma((2,)), dma((FAR,)), dma, dma, dma, dma, dma((Y,)), dma((Y,)),
+            dma((2,)), dma((3,)), dma, dma((Z,)), dma, dma((2,)), dma((len(FAR),)), dma, dma, dma, dma, dma((Y,)), dma((Y,)),
         ],
         compiler_params=pltpu.CompilerParams(
             collective_id=0, has_side_effects=True, vmem_limit_bytes=50 << 20

time: 71.5 us -> 70.7 us (0.989)
  no operation moved by 1% of the time
where the time goes in v2:
time: 70.7 us; the launch traced here: 70.6 us
  Pallas kernels  69.7 us (99%)
  other arithmetic  0.78 us (1%)
    pallas_call x1, Pallas kernels, shards(): pl.pallas_call(body, name='correlate', out_shape=pltpu.VMEM((4, DET, 128)...  68 us
    pallas_call x1, Pallas kernels, shards(): pl.pallas_call(select, name='select', out_shape=jax.ShapeDtypeStruct((MAX...  1.78 us

profile of v2, /device:TPU:24, one launch (start us, length us, event | category | flops | bytes accessed | tf_op | source)
XLA Modules:
  0.0 70.6 jit_solution(2594892626194129405)
XLA Ops:
  0.0 0.0 copy-start.1
  0.0 0.0 copy-start
  0.0 0.8 %select_reduce_fusion.owner_frame = s32[128]{0:T(128)S(1)} fusion(s32[128]{0:T(128)} %bitcast.8), kind=kLoop, calls=%fused_computation | loop fusion | flops 49024 | bytes 1024 | tf_op jit(solution)/shard_map/reduce_sum | solution.py:319
  0.8 68.0 %correlate.1.plane = f32[4,512,128]{2,1,0:T(8,128)S(1)} custom-call(s32[128]{0:T(128)S(1)} %select_reduce_fusion.owner_frame, f32[128,4,512]{2,1,0:T(4,128)} %frames_hbm.1, f32[8,128]{1,0:T(8,128)} %bitcast.7, bf16[2176,256]{1,0:T(8,128)(2,1)} %constant.8.clone.wide_hbm, bf16[3616,512]{1,0:T(8,128)(2,1)} %constant.9.clone.square_hbm, ...), custom_call_target="tpu_custom_call" | custom-call | tf_op jit(solution)/shard_map/correlate/pallas_call | solution.py:329
  68.8 0.0 copy-done.1
  68.8 0.0 copy-done
  68.8 1.8 %select.1 = f32[16,4096]{1,0:T(8,128)} custom-call(s32[128]{0:T(128)S(1)} %select_reduce_fusion.owner_frame, s32[16,128]{1,0:T(8,128)S(1)} %bitcast.6, s32[128]{0:T(128)S(1)} %copy-done.1, f32[4,512,128]{2,1,0:T(8,128)S(1)} %correlate.1.plane), custom_call_target="tpu_custom_call" | custom-call | tf_op jit(solution)/shard_map/select/pallas_call | solution.py:360
Async XLA Ops:
  0.0 68.8 %copy-start.1 = (s32[128]{0:T(128)S(1)}, s32[128]{0:T(128)}, u32[]{:S(2)}) copy-start(s32[128]{0:T(128)} %counts.1) | copy-start | bytes 1540
  0.0 68.8 %copy-start = (s32[128,16]{0,1:T(8,128)S(1)}, s32[128,16]{0,1:T(8,128)}, u32[]{:S(2)}) copy-start(s32[128,16]{0,1:T(8,128)} %param.11) | copy-start | bytes 24580

commit v3 on v2

--- a/solution.py
+++ b/solution.py
@@ -20,7 +20,7 @@
 STRIP = ("z", "x", "c")
 U = 272
 AHEAD = 9
-FAR = (8, 9, 7, 10)
+FAR = (8, 9, 7)
 F32 = jnp.float32
 BF16 = jnp.bfloat16
 MESH = pl.DeviceIdType.MESH
@@ -243,7 +243,7 @@
         return mul(w_high, high) + mul(w_high, low) + mul(w_low, high)
 
     wait_bytes(rows.at[pl.ds(0, len(FAR) * (PLANE - 1))], recv_out)
-    wait_bytes(rows.at[pl.ds(0, 40)], recv_z.at[0])
+    wait_bytes(rows.at[pl.ds(0, 48)], recv_z.at[0])
     spec[...] = over_rows(0)
     wait_bytes(rows.at[pl.ds(0, 48)], recv_z.at[1])
     total = spec[...] + over_rows(1)

time: 70.7 us -> 70.2 us (level)
  no operation moved by 1% of the time
where the time goes in v3:
time: 70.2 us; the launch traced here: 70.1 us
  Pallas kernels  69.2 us (99%)
  other arithmetic  0.78 us (1%)
    pallas_call x1, Pallas kernels, shards(): pl.pallas_call(body, name='correlate', out_shape=pltpu.VMEM((4, DET, 128)...  67.5 us
    pallas_call x1, Pallas kernels, shards(): pl.pallas_call(select, name='select', out_shape=jax.ShapeDtypeStruct((MAX...  1.78 us

profile of v3, /device:TPU:24, one launch (start us, length us, event | category | flops | bytes accessed | tf_op | source)
XLA Modules:
  0.0 70.1 jit_solution(7518230272804304519)
XLA Ops:
  0.0 0.0 copy-start.1
  0.0 0.0 copy-start
  0.0 0.8 %select_reduce_fusion.owner_frame = s32[128]{0:T(128)S(1)} fusion(s32[128]{0:T(128)} %bitcast.8), kind=kLoop, calls=%fused_computation | loop fusion | flops 49024 | bytes 1024 | tf_op jit(solution)/shard_map/reduce_sum | solution.py:319
  0.8 67.5 %correlate.1.plane = f32[4,512,128]{2,1,0:T(8,128)S(1)} custom-call(s32[128]{0:T(128)S(1)} %select_reduce_fusion.owner_frame, f32[128,4,512]{2,1,0:T(4,128)} %frames_hbm.1, f32[8,128]{1,0:T(8,128)} %bitcast.7, bf16[2176,256]{1,0:T(8,128)(2,1)} %constant.8.clone.wide_hbm, bf16[3616,512]{1,0:T(8,128)(2,1)} %constant.9.clone.square_hbm, ...), custom_call_target="tpu_custom_call" | custom-call | tf_op jit(solution)/shard_map/correlate/pallas_call | solution.py:329
  68.3 0.0 copy-done.1
  68.3 0.0 copy-done
  68.3 1.8 %select.1 = f32[16,4096]{1,0:T(8,128)} custom-call(s32[128]{0:T(128)S(1)} %select_reduce_fusion.owner_frame, s32[16,128]{1,0:T(8,128)S(1)} %bitcast.6, s32[128]{0:T(128)S(1)} %copy-done.1, f32[4,512,128]{2,1,0:T(8,128)S(1)} %correlate.1.plane), custom_call_target="tpu_custom_call" | custom-call | tf_op jit(solution)/shard_map/select/pallas_call | solution.py:360
Async XLA Ops:
  0.0 68.3 %copy-start.1 = (s32[128]{0:T(128)S(1)}, s32[128]{0:T(128)}, u32[]{:S(2)}) copy-start(s32[128]{0:T(128)} %counts.1) | copy-start | bytes 1540
  0.0 68.3 %copy-start = (s32[128,16]{0,1:T(8,128)S(1)}, s32[128,16]{0,1:T(8,128)}, u32[]{:S(2)}) copy-start(s32[128,16]{0,1:T(8,128)} %param.11) | copy-start | bytes 24580
